TPU v7x, 32 devices: a whole 2x2x4 slice. The times are simulated.
32 devices in a mesh: groups: 2 (over y), res: 4 (over z), col: 2 (over x), seq: 2 (over core).
Axes of the slice: x: 2, y: 2, z: 4, core: 2. Of those that a mesh axis runs over, the one named last changes fastest.
Arguments:
- alignment_states: bfloat16 [128, 128, 256], P(('groups', 'res', 'seq'), 'col'), parts along dimension 0, may hold values from -6 to 6
- standardize_scale: float32 [256], replicated, may hold values from 0.5 to 1.5
- standardize_shift: float32 [256], replicated, may hold values from -3 to 3
- first_factor_coeffs: bfloat16 [256, 32], replicated, may hold values from -0.375 to 0.375
- first_factor_offset: float32 [32], replicated, may hold values from -3 to 3
- second_factor_coeffs: bfloat16 [256, 32], replicated, may hold values from -0.375 to 0.375
- second_factor_offset: float32 [32], replicated, may hold values from -3 to 3
- final_coeffs: bfloat16 [1024, 128], replicated, may hold values from -0.1875 to 0.1875
- final_offset: float32 [128], replicated, may hold values from -3 to 3
Outputs:
- pair: bfloat16 [4, 64, 128, 128], P('groups', ('res', 'seq'), 'col'), parts along dimension 0
There are 2 independent parts, one for each index of `groups`. A program takes and returns all parts, laid end to end along the dimension named above; an argument that names none is the same for every part. Nothing has to cross between parts.
All inputs are finite; a program needn't handle non-finite values.
Results may differ from a plain program's by a relative error of at most 0.0037.
Values may be sent and summed in bfloat16 or wider, within the bound.
A program may use at most 64 MiB of HBM per device.

v0:
```python
import jax
import jax.numpy as jnp
from jax import lax
from jax.sharding import PartitionSpec as P


def project_both(rows, standardize_scale, standardize_shift, w_both, bias_both):
    input_tensor = rows.astype(jnp.float32)
    mean = jnp.mean(input_tensor, axis=-1, keepdims=True)
    centred = input_tensor - mean
    variance = jnp.mean(centred * centred, axis=-1, keepdims=True)
    normed = (centred * lax.rsqrt(variance + 1e-05) * standardize_scale + standardize_shift).astype(
        jnp.bfloat16
    )
    return (jnp.dot(normed, w_both, preferred_element_type=jnp.float32) + bias_both).astype(
        jnp.bfloat16
    )


def per_device(
    alignment_states,
    standardize_scale,
    standardize_shift,
    first_factor_coeffs,
    first_factor_offset,
    second_factor_coeffs,
    second_factor_offset,
    final_coeffs,
    final_offset,
):
    aligned_rows_each_shard, position_span, hidden_dimension = alignment_states.shape
    position_number = lax.axis_size("res")
    n_seq = lax.axis_size("seq")
    n_col = lax.axis_size("col")
    positions_each_shard = position_span // position_number
    chans = first_factor_coeffs.shape[1]
    seq_loc = aligned_rows_each_shard * position_number
    w_both = jnp.concatenate([first_factor_coeffs, second_factor_coeffs], axis=1)
    bias_both = jnp.concatenate([first_factor_offset, second_factor_offset])
    raw = lax.all_to_all(
        alignment_states.reshape(
            aligned_rows_each_shard, position_number, positions_each_shard * hidden_dimension
        ),
        "res",
        split_axis=1,
        concat_axis=0,
        tiled=True,
    )
    both = project_both(
        raw.reshape(seq_loc * positions_each_shard, hidden_dimension),
        standardize_scale,
        standardize_shift,
        w_both,
        bias_both,
    )
    both = both.reshape(seq_loc, positions_each_shard, 2 * chans)
    left_loc = both[:, :, :chans].reshape(seq_loc, positions_each_shard * chans)
    right_three = both[:, :, chans:]
    right_loc = right_three.transpose(1, 0, 2).reshape(positions_each_shard, seq_loc * chans)
    left_use = lax.all_to_all(left_loc, "seq", split_axis=1, concat_axis=0, tiled=True)
    right_use = lax.all_gather(right_loc, "seq", axis=1, tiled=True)
    rows_all = lax.all_gather(left_use, "col", axis=1, tiled=True)
    seqs = rows_all.shape[0]
    per_group = seqs // n_seq
    n_rows = rows_all.shape[1] // chans
    left_four = rows_all.reshape(n_seq, per_group, n_rows, chans)
    pair_width = final_coeffs.shape[1]
    w_deep = jnp.concatenate([final_coeffs] * n_seq, axis=0)

    def one_block(block):
        sub = block.shape[0]
        block = block.reshape(sub, n_seq, per_group, chans)
        outer = jnp.einsum("gsic,jgse->ijgce", left_four, block, preferred_element_type=jnp.float32)
        outer = outer.astype(jnp.bfloat16).reshape(n_rows * sub, n_seq * chans * chans)
        summed = jnp.dot(outer, w_deep, preferred_element_type=jnp.float32)
        return summed.reshape(n_rows, sub, pair_width)

    piece = lax.all_gather(right_use, "res", axis=0, tiled=True)
    count = piece.shape[0]
    sub = 1
    for option in range(1, 17):
        if count % option == 0:
            sub = option
    blocks = piece.reshape(count // sub, sub, piece.shape[1])
    results = lax.map(one_block, blocks)
    summed = results.transpose(1, 0, 2, 3).reshape(n_rows, count, pair_width)
    summed = summed.reshape(n_col, n_rows // n_col, summed.shape[1], pair_width)
    total = float(aligned_rows_each_shard * position_number * n_seq)
    return (summed / total + final_offset).astype(jnp.bfloat16)


def solution(mesh):
    return jax.shard_map(
        per_device,
        mesh=mesh,
        in_specs=(P(("groups", "res", "seq"), "col", None), P(), P(), P(), P(), P(), P(), P(), P()),
        out_specs=P("groups", ("res", "seq"), "col", None),
        check_vma=False,
    )
```

profile of v0, /device:TPU:0, one launch (start us, length us, event | category | flops | bytes accessed | tf_op | source)
XLA Modules:
  0.0 109.3 jit_solution(5657845986276746612)
XLA Ops:
  0.0 1.2 %reshape.58 = bf16[8,4,4096]{2,1,0:T(4,128)(2,1)S(1)} reshape(bf16[8,64,256]{2,1,0:T(8,128)(2,1)} %param.11) | data formatting | bytes 524288 | tf_op jit(solution)/shard_map/reshape | solution.py:41
  1.2 0.9 copy.21
  2.0 6.4 %all-to-all-start = ((bf16[8,4,4096]{2,0,1:T(8,128)(2,1)}), bf16[8,4,4096]{2,0,1:T(8,128)(2,1)S(1)}, u32[]{:S(2)}, u32[]{:S(2)}) async-start(bf16[8,4,4096]{2,0,1:T(8,128)(2,1)} %copy.21), calls=%async_computation | async-start | bytes 524288 | tf_op jit(solution)/shard_map/all_to_all | solution.py:40
  8.4 0.7 pad_maximum_fusion.1
  9.2 1.1 pad_maximum_fusion
  10.2 7.1 %all-to-all-done = bf16[8,4,4096]{2,0,1:T(8,128)(2,1)S(1)} async-done(((bf16[8,4,4096]{2,0,1:T(8,128)(2,1)}), bf16[8,4,4096]{2,0,1:T(8,128)(2,1)S(1)}, u32[]{:S(2)}, u32[]{:S(2)}) %all-to-all-start) | async-done | bytes 262176 | tf_op jit(solution)/shard_map/all_to_all | solution.py:40
  18.6 3.7 %all_to_all.28 = bf16[32,2,256]{2,0,1:T(8,128)(2,1)S(1)} all-to-all(bf16[32,2,256]{2,0,1:T(8,128)(2,1)S(1)} %copy.24), channel_id=1, replica_groups=mesh['groups'=2,'res'=4,'col'=2,'seq'=2] {'seq'}, dimensions={1} | all-to-all | bytes 65536 | tf_op jit(solution)/shard_map/all_to_all | solution.py:60
  22.4 4.6 %all_gather.11 = bf16[64,512]{1,0:T(8,128)(2,1)S(1)} all-gather(bf16[64,256]{1,0:T(8,128)(2,1)S(1)} %bitcast.55), channel_id=1, replica_groups=mesh['groups'=2,'res'=4,'col'=2,'seq'=2] {'col'}, dimensions={1}, use_global_device_ids=true | all-gather | bytes 98304 | tf_op jit(solution)/shard_map/all_gather | solution.py:62
  27.4 1.9 %all_gather.9 = bf16[16,2048]{1,0:T(8,128)(2,1)S(1)} all-gather(bf16[16,1024]{1,0:T(8,128)(2,1)S(1)} %reshape.60), channel_id=1, replica_groups=mesh['groups'=2,'res'=4,'col'=2,'seq'=2] {'seq'}, dimensions={1}, use_global_device_ids=true | all-gather | bytes 98304 | tf_op jit(solution)/shard_map/all_gather | solution.py:61
  29.3 13.8 %all_gather.10 = bf16[64,2048]{1,0:T(8,128)(2,1)S(1)} all-gather(bf16[16,2048]{1,0:T(8,128)(2,1)S(1)} %all_gather.9), channel_id=1, replica_groups=mesh['groups'=2,'res'=4,'col'=2,'seq'=2] {'res'}, dimensions={0}, use_global_device_ids=true | all-gather | bytes 327680 | tf_op jit(solution)/shard_map/all_gather | solution.py:78
  43.1 65.3 %while.10 = (s32[]{:T(128)}, f32[4,16,16,128]{3,2,1,0:T(8,128)S(1)}, bf16[4,16,2048]{2,1,0:T(8,128)(2,1)S(1)}, bf16[2,32,16,32]{3,1,2,0:T(8,128)(2,1)S(1)}, bf16[2048,128]{1,0:T(8,128)(2,1)S(1)}, /*index=5*/s32[]{:T(128)}) while((s32[]{:T(128)}, f32[4,16,16,128]{3,2,1,0:T(8,128)S(1)}, bf16[4,16,2048]{2,1,0:T(8,128)(2,1)S(1)}, ...), condition=%wide.region_3.4_spmd, body=%wide.region_2.3_spmd.sunk | while | flops 168296448 | bytes 7340109 | solution.py:85
  43.3 3.2 %convert_bitcast_fusion.3 = bf16[16,16,2,32,32]{3,4,0,1,2:T(8,128)(2,1)} fusion(bf16[2,32,16,32]{3,1,2,0:T(8,128)(2,1)S(1)} %get-tuple-element.101, bf16[16,2,32,32]{3,2,1,0:T(8,128)(2,1)S(1)} %reshape.70), kind=kOutput, calls=%fused_computation.clone.1 | convolution fusion | flops 34078720 | bytes 1179648 | tf_op jit(solution)/shard_map/while/body/eval_jaxpr/gsic,jgse->ijgce/dot_general | solution.py:73
  46.5 6.4 %copy.36 = bf16[16,16,2,32,32]{4,3,2,1,0:T(8,128)(2,1)} copy(bf16[16,16,2,32,32]{3,4,0,1,2:T(8,128)(2,1)} %convert_bitcast_fusion.3) | data formatting | bytes 2097152 | tf_op jit(solution)/shard_map/while/body/eval_jaxpr/convert_element_type | solution.py:74
  53.0 6.0 %reshape.71 = bf16[16,16,2048]{2,1,0:T(8,128)(2,1)S(1)} reshape(bf16[16,16,2,32,32]{4,3,2,1,0:T(8,128)(2,1)} %copy.36) | data formatting | bytes 2097152 | tf_op jit(solution)/shard_map/reshape.23
  59.6 3.2 %convert_bitcast_fusion.3 = bf16[16,16,2,32,32]{3,4,0,1,2:T(8,128)(2,1)} fusion(bf16[2,32,16,32]{3,1,2,0:T(8,128)(2,1)S(1)} %get-tuple-element.101, bf16[16,2,32,32]{3,2,1,0:T(8,128)(2,1)S(1)} %reshape.70), kind=kOutput, calls=%fused_computation.clone.1 | convolution fusion | flops 34078720 | bytes 1179648 | tf_op jit(solution)/shard_map/while/body/eval_jaxpr/gsic,jgse->ijgce/dot_general | solution.py:73
  62.9 6.4 %copy.36 = bf16[16,16,2,32,32]{4,3,2,1,0:T(8,128)(2,1)} copy(bf16[16,16,2,32,32]{3,4,0,1,2:T(8,128)(2,1)} %convert_bitcast_fusion.3) | data formatting | bytes 2097152 | tf_op jit(solution)/shard_map/while/body/eval_jaxpr/convert_element_type | solution.py:74
  69.3 6.0 %reshape.71 = bf16[16,16,2048]{2,1,0:T(8,128)(2,1)S(1)} reshape(bf16[16,16,2,32,32]{4,3,2,1,0:T(8,128)(2,1)} %copy.36) | data formatting | bytes 2097152 | tf_op jit(solution)/shard_map/reshape.23
  76.0 3.2 %convert_bitcast_fusion.3 = bf16[16,16,2,32,32]{3,4,0,1,2:T(8,128)(2,1)} fusion(bf16[2,32,16,32]{3,1,2,0:T(8,128)(2,1)S(1)} %get-tuple-element.101, bf16[16,2,32,32]{3,2,1,0:T(8,128)(2,1)S(1)} %reshape.70), kind=kOutput, calls=%fused_computation.clone.1 | convolution fusion | flops 34078720 | bytes 1179648 | tf_op jit(solution)/shard_map/while/body/eval_jaxpr/gsic,jgse->ijgce/dot_general | solution.py:73
  79.2 6.4 %copy.36 = bf16[16,16,2,32,32]{4,3,2,1,0:T(8,128)(2,1)} copy(bf16[16,16,2,32,32]{3,4,0,1,2:T(8,128)(2,1)} %convert_bitcast_fusion.3) | data formatting | bytes 2097152 | tf_op jit(solution)/shard_map/while/body/eval_jaxpr/convert_element_type | solution.py:74
  85.6 6.0 %reshape.71 = bf16[16,16,2048]{2,1,0:T(8,128)(2,1)S(1)} reshape(bf16[16,16,2,32,32]{4,3,2,1,0:T(8,128)(2,1)} %copy.36) | data formatting | bytes 2097152 | tf_op jit(solution)/shard_map/reshape.23
  92.3 3.2 %convert_bitcast_fusion.3 = bf16[16,16,2,32,32]{3,4,0,1,2:T(8,128)(2,1)} fusion(bf16[2,32,16,32]{3,1,2,0:T(8,128)(2,1)S(1)} %get-tuple-element.101, bf16[16,2,32,32]{3,2,1,0:T(8,128)(2,1)S(1)} %reshape.70), kind=kOutput, calls=%fused_computation.clone.1 | convolution fusion | flops 34078720 | bytes 1179648 | tf_op jit(solution)/shard_map/while/body/eval_jaxpr/gsic,jgse->ijgce/dot_general | solution.py:73
  95.5 6.4 %copy.36 = bf16[16,16,2,32,32]{4,3,2,1,0:T(8,128)(2,1)} copy(bf16[16,16,2,32,32]{3,4,0,1,2:T(8,128)(2,1)} %convert_bitcast_fusion.3) | data formatting | bytes 2097152 | tf_op jit(solution)/shard_map/while/body/eval_jaxpr/convert_element_type | solution.py:74
  102.0 6.0 %reshape.71 = bf16[16,16,2048]{2,1,0:T(8,128)(2,1)S(1)} reshape(bf16[16,16,2,32,32]{4,3,2,1,0:T(8,128)(2,1)} %copy.36) | data formatting | bytes 2097152 | tf_op jit(solution)/shard_map/reshape.23
  108.5 0.8 add_convert_fusion
  (40 shorter events, 4.3 us)
Async XLA Ops:
  0.0 17.9 %copy-start.4 = (f32[256]{0:T(256)S(1)}, f32[256]{0:T(256)}, u32[]{:S(2)}) copy-start(f32[256]{0:T(256)} %param.12) | copy-start | bytes 3076
  0.0 17.9 %copy-start.3 = (f32[256]{0:T(256)S(1)}, f32[256]{0:T(256)}, u32[]{:S(2)}) copy-start(f32[256]{0:T(256)} %param.13) | copy-start | bytes 3076
  0.0 17.9 %copy-start.2 = (bf16[256,32]{0,1:T(8,128)(2,1)S(1)}, bf16[256,32]{0,1:T(8,128)(2,1)}, u32[]{:S(2)}) copy-start(bf16[256,32]{0,1:T(8,128)(2,1)} %param.14) | copy-start | bytes 49156
  0.0 17.9 %copy-start.1 = (bf16[256,32]{0,1:T(8,128)(2,1)S(1)}, bf16[256,32]{0,1:T(8,128)(2,1)}, u32[]{:S(2)}) copy-start(bf16[256,32]{0,1:T(8,128)(2,1)} %param.16) | copy-start | bytes 49156
  2.0 15.3 %all-to-all-start = ((bf16[8,4,4096]{2,0,1:T(8,128)(2,1)}), bf16[8,4,4096]{2,0,1:T(8,128)(2,1)S(1)}, u32[]{:S(2)}, u32[]{:S(2)}) async-start(bf16[8,4,4096]{2,0,1:T(8,128)(2,1)} %copy.21), calls=%async_computation | async-start | bytes 524288 | tf_op jit(solution)/shard_map/all_to_all | solution.py:40
  43.1 65.4 %copy-start = (f32[128]{0:T(128)S(1)}, f32[128]{0:T(128)}, u32[]{:S(2)}) copy-start(f32[128]{0:T(128)} %param.19) | copy-start | bytes 1540
where the time goes:
time: 110 us; the launch traced here: 109 us
  local copies, waits for them, and re-layouts  53.6 us (49%)
  blocking collectives  24 us (22%)
  matrix products  15 us (14%)
  waiting for transfers between devices  7.1 us (6%)
  starting transfers between devices  6.36 us (6%)
  other arithmetic  3.04 us (3%)
    convert_element_type x4, local copies, waits for them, and re-layouts, one_block(): outer.astype(jnp.bfloat16).reshape(n_rows * sub, n_seq * chans * chans)  25.8 us
    another operation x4, local copies, waits for them, and re-layouts  24 us
    all_gather x1, blocking collectives, per_device(): piece = lax.all_gather(right_use, 'res', axis=0, tiled=True)  13.8 us
    dot_general x4, matrix products, one_block(): jnp.einsum('gsic,jgse->ijgce', left_four, block, preferred_element_type=j...  12.9 us
    all_to_all x1, waiting for transfers between devices, per_device(): lax.all_to_all(alignment_states.reshape(aligned_rows_each_shard, position...  7.1 us
    all_to_all x1, starting transfers between devices, per_device(): lax.all_to_all(alignment_states.reshape(aligned_rows_each_shard, position...  6.36 us
    all_gather x1, blocking collectives, per_device(): rows_all = lax.all_gather(left_use, 'col', axis=1, tiled=True)  4.57 us
    all_to_all x1, blocking collectives, per_device(): lax.all_to_all(left_loc, 'seq', split_axis=1, concat_axis=0, tiled=True)  3.75 us
  transfers between devices with their start and end apart: 1, of which 1 were waited for; matrix products, arithmetic and copies ran while one was open for 2% of the time, Pallas kernels for 0%

commit v1 on v0

v1 whole, which is shorter than its diff:
```python
import functools

import jax
import jax.numpy as jnp
from jax import lax
from jax.experimental import pallas as pl
from jax.experimental.pallas import tpu as pltpu
from jax.sharding import PartitionSpec as P

MESH = pl.DeviceIdType.MESH
F32 = jnp.float32
BF16 = jnp.bfloat16


def one_hot(shape, wanted):
    row = lax.broadcasted_iota(jnp.int32, shape, 0)
    col = lax.broadcasted_iota(jnp.int32, shape, 1)
    return jnp.where(wanted(row, col), 1.0, 0.0)


def column_of(row, size):
    spread = jnp.broadcast_to(row, (size, size))
    return jnp.sum(one_hot((size, size), lambda r, c: r == c) * spread, axis=1, keepdims=True)


def matmul(a, b):
    return jnp.dot(a, b, preferred_element_type=F32)


def kernel(
    dims,
    msa,
    scale,
    shift,
    w_left,
    b_left,
    w_right,
    b_right,
    w_hbm,
    b_out,
    out,
    w_vmem,
    w_f32,
    w_flip,
    both_s,
    turn_s,
    left_send,
    left_all,
    left_flip,
    right_all,
    outer,
    w_sem,
    left_ssem,
    left_rsem,
    right_ssem,
    right_rsem,
):
    n_res, n_col, n_seq, seqs, span, width, chans, pairs = dims
    n_src = n_res * n_seq
    n_all = n_src * n_col
    fold = max(1, 128 // span)
    high = chans // fold
    rows = span // n_src
    lanes = fold * span
    group = outer.shape[2] // lanes
    res, col, seq = lax.axis_index("res"), lax.axis_index("col"), lax.axis_index("seq")
    src = res * n_seq + seq
    me = col * n_src + src

    def place(index):
        at = lax.rem(index, n_src)
        return {"res": at // n_seq, "col": index // n_src, "seq": lax.rem(at, n_seq)}

    def each(count, body):
        if count <= 16:
            for step in range(1, count):
                body(step)
        else:
            lax.fori_loop(1, count, lambda step, _: (body(step), 0)[1], 0)

    barrier = pltpu.get_barrier_semaphore()

    def greet(step):
        pl.semaphore_signal(barrier, inc=1, device_id=place(lax.rem(me + step, n_all)), device_id_type=MESH)

    each(n_all, greet)
    w_copy = pltpu.make_async_copy(w_hbm, w_vmem, w_sem)
    w_copy.start()

    w_both = jnp.concatenate([w_left[...], w_right[...]], axis=1)
    b_both = jnp.concatenate([b_left[...], b_right[...]], axis=1)
    for s in range(seqs):
        x = msa[s].astype(F32)
        mean = jnp.mean(x, axis=-1, keepdims=True)
        centred = x - mean
        variance = jnp.mean(centred * centred, axis=-1, keepdims=True)
        normed = (centred * lax.rsqrt(variance + 1e-05) * scale[...] + shift[...]).astype(BF16)
        both = matmul(normed, w_both) + b_both
        both_s[pl.ds(s * span, span), :] = both
        pick = one_hot(
            (chans, 2 * chans), lambda r, c: c == chans + lax.rem(r, high) * fold + r // high
        ).astype(BF16)
        turned = lax.dot_general(
            pick, both.astype(BF16), (((1,), (1,)), ((), ())), preferred_element_type=F32
        )
        parts = [turned[k * high : (k + 1) * high] for k in range(fold)]
        whole = parts[0] if fold == 1 else jnp.concatenate(parts, axis=1)
        for k in range(lanes // 128):
            turn_s[k, pl.ds(s * high, high), :] = whole[:, k * 128 : (k + 1) * 128]

    for e in range(high):
        for k in range(lanes // 128):
            right_all[src, e, :, pl.ds(k * 128, 128)] = turn_s[
                k, pl.ds(e, seqs, stride=high), :
            ].astype(BF16)

    total = None
    for v in range(rows):
        got = jnp.concatenate(
            [both_s[pl.ds(b * rows + v, seqs, stride=span), :] for b in range(n_src)], axis=0
        )
        spot = one_hot(
            (2 * chans, rows * chans), lambda r, c: (c == v * chans + r) & (r < chans)
        ).astype(BF16)
        term = matmul(got.astype(BF16), spot)
        total = term if total is None else total + term
    total = total.reshape(n_src, seqs, rows * chans).astype(BF16)
    left_send[...] = total

    pl.semaphore_wait(barrier, n_all - 1)

    def left_copy(step):
        to = lax.rem(me + step, n_all)
        return pltpu.make_async_remote_copy(
            src_ref=left_send.at[lax.rem(to, n_src)],
            dst_ref=left_all.at[me],
            send_sem=left_ssem.at[step],
            recv_sem=left_rsem.at[step],
            device_id=place(to),
            device_id_type=MESH,
        )

    def right_copy(step):
        to = lax.rem(src + step, n_src)
        return pltpu.make_async_remote_copy(
            src_ref=right_all.at[src],
            dst_ref=right_all.at[src],
            send_sem=right_ssem.at[step],
            recv_sem=right_rsem.at[step],
            device_id=place(col * n_src + to),
            device_id_type=MESH,
        )

    each(n_all, lambda step: left_copy(step).start())
    each(n_src, lambda step: right_copy(step).start())
    left_all[me] = left_send[src]

    w_copy.wait()
    w_f32[...] = w_vmem[...].astype(F32)
    chunk = 4
    for at in range(0, chans, chunk):
        taken = jnp.concatenate(
            [w_f32[pl.ds(e, chans, stride=chans), :] for e in range(at, at + chunk)], axis=0
        )
        w_flip[:, pl.ds(at * chans, chunk * chans)] = taken.T.astype(BF16)
    offset = column_of(b_out[...], pairs)

    each(n_all, lambda step: left_copy(step).wait())
    deep = fold * n_src * seqs
    for u in range(n_col // fold):
        taken = left_all[pl.ds(u * fold * n_src, fold * n_src)].astype(F32)
        left_flip[u] = taken.reshape(deep, rows * chans).T.astype(BF16)
    each(n_src, lambda step: right_copy(step).wait())

    factor = 1.0 / float(seqs * n_src)
    for u in range(n_col // fold):
        left = left_flip[u]
        for h in range(high):
            block = right_all[:, h].astype(F32).reshape(n_src * seqs, lanes)
            if fold == 1:
                wide = block
            else:
                lane = lax.broadcasted_iota(jnp.int32, block.shape, 1) // span
                columns = []
                for k in range(fold):
                    tall = []
                    for t in range(fold):
                        moved = block if t == k else pltpu.roll(block, ((t - k) % fold) * span, 1)
                        tall.append(jnp.where(lane == t, moved, 0.0))
                    columns.append(jnp.concatenate(tall, axis=0))
                wide = jnp.concatenate(columns, axis=1)
            product = matmul(left, wide.astype(BF16)).astype(BF16)
            for k in range(fold):
                for v in range(rows):
                    outer[
                        v // group,
                        pl.ds((h * fold + k) * chans, chans),
                        pl.ds((v % group) * lanes, lanes),
                    ] = product[v * chans : (v + 1) * chans, k * lanes : (k + 1) * lanes]
        for g in range(rows // group):
            summed = matmul(w_flip[...], outer[g])
            done = (summed * factor + offset).astype(BF16).T
            for k in range(group):
                for t in range(fold):
                    out[u * fold + t, g * group + k] = done[
                        k * lanes + t * span : k * lanes + (t + 1) * span
                    ]


def per_device(msa, scale, shift, w_left, b_left, w_right, b_right, w_out, b_out):
    seqs, span, width = msa.shape
    n_res, n_col, n_seq = lax.axis_size("res"), lax.axis_size("col"), lax.axis_size("seq")
    chans = w_left.shape[1]
    pairs = w_out.shape[1]
    n_src = n_res * n_seq
    fold = max(1, 128 // span)
    high = chans // fold
    rows = span // n_src
    lanes = fold * span
    group = max(1, 256 // lanes)
    deep = fold * n_src * seqs
    dims = (n_res, n_col, n_seq, seqs, span, width, chans, pairs)
    vmem = pl.BlockSpec(memory_space=pltpu.VMEM)
    return pl.pallas_call(
        functools.partial(kernel, dims),
        out_shape=jax.ShapeDtypeStruct((n_col, rows, span, pairs), BF16),
        in_specs=[vmem] * 7 + [pl.BlockSpec(memory_space=pl.ANY), vmem],
        out_specs=vmem,
        scratch_shapes=[
            pltpu.VMEM(w_out.shape, BF16),
            pltpu.VMEM(w_out.shape, F32),
            pltpu.VMEM((pairs, chans * chans), BF16),
            pltpu.VMEM((seqs * span, 2 * chans), F32),
            pltpu.VMEM((lanes // 128, seqs * high, 128), F32),
            pltpu.VMEM((n_src, seqs, rows * chans), BF16),
            pltpu.VMEM((n_src * n_col, seqs, rows * chans), BF16),
            pltpu.VMEM((n_col // fold, rows * chans, deep), BF16),
            pltpu.VMEM((n_src, high, seqs, lanes), BF16),
            pltpu.VMEM((rows // group, chans * chans, group * lanes), BF16),
            pltpu.SemaphoreType.DMA,
            pltpu.SemaphoreType.DMA((n_src * n_col,)),
            pltpu.SemaphoreType.DMA((n_src * n_col,)),
            pltpu.SemaphoreType.DMA((n_src,)),
            pltpu.SemaphoreType.DMA((n_src,)),
        ],
        compiler_params=pltpu.CompilerParams(collective_id=0, has_side_effects=True),
    )(
        msa,
        scale.reshape(1, width),
        shift.reshape(1, width),
        w_left,
        b_left.reshape(1, chans),
        w_right,
        b_right.reshape(1, chans),
        w_out,
        b_out.reshape(1, pairs),
    )


def solution(mesh):
    return jax.shard_map(
        per_device,
        mesh=mesh,
        in_specs=(P(("groups", "res", "seq"), "col", None), P(), P(), P(), P(), P(), P(), P(), P()),
        out_specs=P("groups", ("res", "seq"), "col", None),
        check_vma=False,
    )
```

time: 110 us -> 20.1 us (0.18)
  local copies, waits for them, and re-layouts: 53.6 us -> 3.86 us
  blocking collectives: 24 us -> 0 us
  Pallas kernels: 0 us -> 15.9 us
  matrix products: 15 us -> 0 us
  waiting for transfers between devices: 7.1 us -> 0 us
  starting transfers between devices: 6.36 us -> 0 us
  other arithmetic: 3.04 us -> 0 us
    convert_element_type x6 -> x0, local copies, waits for them, and re-layouts: 26 us -> none  [the longest x4 25.8 us: one_block(): outer.astype(jnp.bfloat16).reshape(n_rows * sub, n_seq * chans * chans)]
    another operation x4 -> x0, local copies, waits for them, and re-layouts: 24 us -> none
    all_gather x3 -> x0, blocking collectives: 20.2 us -> none  [the longest x1 13.8 us: per_device(): piece = lax.all_gather(right_use, 'res', axis=0, tiled=True)]
    pallas_call x0 -> x1, Pallas kernels: none -> 15.9 us  [per_device(): pl.pallas_call(functools.partial(kernel, dims), out_shape=jax.ShapeDtypeS...]
    dot_general x9 -> x0, matrix products: 15 us -> none  [the longest x4 12.9 us: one_block(): jnp.einsum('gsic,jgse->ijgce', left_four, block, preferred_element_type=j...]
    all_to_all x1 -> x0, waiting for transfers between devices: 7.1 us -> none  [per_device(): lax.all_to_all(alignment_states.reshape(aligned_rows_each_shard, position...]
    all_to_all x1 -> x0, starting transfers between devices: 6.36 us -> none  [per_device(): lax.all_to_all(alignment_states.reshape(aligned_rows_each_shard, position...]
    unnamed x10 -> x5, local copies, waits for them, and re-layouts: 0.02 us -> 3.86 us
  transfers between devices with their start and end apart: 1 -> 0, of which waited for: 1 -> 0; matrix products, arithmetic and copies ran while one was open for 2% -> 0% of each run, Pallas kernels for 0% -> 0%
where the time goes in v1:
time: 20.1 us; the launch traced here: 19.8 us
  Pallas kernels  15.9 us (79%)
  local copies, waits for them, and re-layouts  3.86 us (19%)
    pallas_call x1, Pallas kernels, per_device(): pl.pallas_call(functools.partial(kernel, dims), out_shape=jax.ShapeDtypeS...  15.9 us
    unnamed x5, local copies, waits for them, and re-layouts  3.86 us

profile of v1, /device:TPU:0, one launch (start us, length us, event | category | flops | bytes accessed | tf_op | source)
XLA Modules:
  0.0 19.8 jit_solution(17088970629289921874)
XLA Ops:
  0.0 0.0 copy-start
  0.0 1.5 %copy.10.w_left = bf16[256,32]{1,0:T(8,128)(2,1)} copy(bf16[256,32]{0,1:T(8,128)(2,1)} %param.12) | data formatting | bytes 32768 | tf_op args[3]
  1.5 0.0 copy-done
  1.5 0.7 %copy.11.w_right = bf16[256,32]{1,0:T(8,128)(2,1)} copy(bf16[256,32]{0,1:T(8,128)(2,1)S(1)} %copy-done) | data formatting | bytes 32768 | tf_op args[5]
  2.2 15.9 %shard_map.91 = bf16[2,8,64,128]{3,2,1,0:T(8,128)(2,1)} custom-call(bf16[8,64,256]{2,1,0:T(8,128)(2,1)} %msa.1, f32[1,256]{1,0:T(1,128)} %bitcast.5, f32[1,256]{1,0:T(1,128)} %bitcast.6, bf16[256,32]{1,0:T(8,128)(2,1)} %copy.10.w_left, f32[1,32]{1,0:T(1,128)} %bitcast.7, bf16[256,32]{1,0:T(8,128)(2,1)} %copy.11.w_right, f32[1,32]{1,0:T(1,128)} %bitcast.8, ...), custom_call_target="tpu_custom_call" | custom-call | tf_op jit(solution)/shard_map/pallas_call | solution.py:224
  18.1 1.7 %copy.13 = bf16[2,8,64,128]{3,2,1,0:T(8,128)(2,1)} copy(bf16[2,8,64,128]{3,2,1,0:T(8,128)(2,1)} %shard_map.91) | data formatting | bytes 524288
Async XLA Ops:
  0.0 1.5 %copy-start = (bf16[256,32]{0,1:T(8,128)(2,1)S(1)}, bf16[256,32]{0,1:T(8,128)(2,1)}, u32[]{:S(2)}) copy-start(bf16[256,32]{0,1:T(8,128)(2,1)} %param.14) | copy-start | bytes 49156

commit v2 on v1

--- a/solution.py
+++ b/solution.py
@@ -25,6 +25,10 @@
 
 def matmul(a, b):
     return jnp.dot(a, b, preferred_element_type=F32)
+
+
+def matmul_turned(a, b):
+    return lax.dot_general(a, b, (((1,), (1,)), ((), ())), preferred_element_type=F32)
 
 
 def kernel(
@@ -87,7 +91,7 @@
     w_copy = pltpu.make_async_copy(w_hbm, w_vmem, w_sem)
     w_copy.start()
 
-    w_both = jnp.concatenate([w_left[...], w_right[...]], axis=1)
+    w_both = jnp.concatenate([w_left[...], w_right[...]], axis=0)
     b_both = jnp.concatenate([b_left[...], b_right[...]], axis=1)
     for s in range(seqs):
         x = msa[s].astype(F32)
@@ -95,14 +99,12 @@
         centred = x - mean
         variance = jnp.mean(centred * centred, axis=-1, keepdims=True)
         normed = (centred * lax.rsqrt(variance + 1e-05) * scale[...] + shift[...]).astype(BF16)
-        both = matmul(normed, w_both) + b_both
+        both = matmul_turned(normed, w_both) + b_both
         both_s[pl.ds(s * span, span), :] = both
         pick = one_hot(
             (chans, 2 * chans), lambda r, c: c == chans + lax.rem(r, high) * fold + r // high
         ).astype(BF16)
-        turned = lax.dot_general(
-            pick, both.astype(BF16), (((1,), (1,)), ((), ())), preferred_element_type=F32
-        )
+        turned = matmul_turned(pick, both.astype(BF16))
         parts = [turned[k * high : (k + 1) * high] for k in range(fold)]
         whole = parts[0] if fold == 1 else jnp.concatenate(parts, axis=1)
         for k in range(lanes // 128):
@@ -223,7 +225,7 @@
     vmem = pl.BlockSpec(memory_space=pltpu.VMEM)
     return pl.pallas_call(
         functools.partial(kernel, dims),
-        out_shape=jax.ShapeDtypeStruct((n_col, rows, span, pairs), BF16),
+        out_shape=pltpu.VMEM((n_col, rows, span, pairs), BF16),
         in_specs=[vmem] * 7 + [pl.BlockSpec(memory_space=pl.ANY), vmem],
         out_specs=vmem,
         scratch_shapes=[
@@ -248,9 +250,9 @@
         msa,
         scale.reshape(1, width),
         shift.reshape(1, width),
-        w_left,
+        w_left.T,
         b_left.reshape(1, chans),
-        w_right,
+        w_right.T,
         b_right.reshape(1, chans),
         w_out,
         b_out.reshape(1, pairs),

time: 20.1 us -> 16.1 us (0.80)
  local copies, waits for them, and re-layouts: 3.86 us -> 0.71 us
  Pallas kernels: 15.9 us -> 15.2 us
    unnamed x5 -> x1, local copies, waits for them, and re-layouts: 3.86 us -> 0.71 us
    pallas_call x1, Pallas kernels: 15.9 us -> 15.2 us  [per_device(): pl.pallas_call(functools.partial(kernel, dims), out_shape=pltpu.VMEM((n_c...]
where the time goes in v2:
time: 16.1 us; the launch traced here: 15.9 us
  Pallas kernels  15.2 us (94%)
  local copies, waits for them, and re-layouts  0.71 us (4%)
    pallas_call x1, Pallas kernels, per_device(): pl.pallas_call(functools.partial(kernel, dims), out_shape=pltpu.VMEM((n_c...  15.2 us
    unnamed x1, local copies, waits for them, and re-layouts  0.71 us

profile of v2, /device:TPU:0, one launch (start us, length us, event | category | flops | bytes accessed | tf_op | source)
XLA Modules:
  0.0 15.9 jit_solution(14626361379323793296)
XLA Ops:
  0.0 15.2 %shard_map.91 = bf16[2,8,64,128]{3,2,1,0:T(8,128)(2,1)S(1)} custom-call(bf16[8,64,256]{2,1,0:T(8,128)(2,1)} %msa.1, f32[1,256]{1,0:T(1,128)} %bitcast.9, f32[1,256]{1,0:T(1,128)} %bitcast.10, bf16[32,256]{1,0:T(8,128)(2,1)} %bitcast.7, f32[1,32]{1,0:T(1,128)} %bitcast.11, bf16[32,256]{1,0:T(8,128)(2,1)} %bitcast.8, f32[1,32]{1,0:T(1,128)} %bitcast.12, ...), custom_call_target="tpu_custom_call" | custom-call | tf_op jit(solution)/shard_map/pallas_call | solution.py:226
  15.2 0.7 %copy.11 = bf16[2,8,64,128]{3,2,1,0:T(8,128)(2,1)} copy(bf16[2,8,64,128]{3,2,1,0:T(8,128)(2,1)S(1)} %shard_map.91) | data formatting | bytes 524288

commit v3 on v2

--- a/solution.py
+++ b/solution.py
@@ -142,19 +142,26 @@
             device_id_type=MESH,
         )
 
-    def right_copy(step):
-        to = lax.rem(src + step, n_src)
+    def right_copy(slot, sem, to):
         return pltpu.make_async_remote_copy(
-            src_ref=right_all.at[src],
-            dst_ref=right_all.at[src],
-            send_sem=right_ssem.at[step],
-            recv_sem=right_rsem.at[step],
-            device_id=place(col * n_src + to),
+            src_ref=right_all.at[slot],
+            dst_ref=right_all.at[slot],
+            send_sem=right_ssem.at[sem],
+            recv_sem=right_rsem.at[sem],
+            device_id=to,
             device_id_type=MESH,
         )
 
+    def far(step):
+        return right_copy(src, step, {"res": lax.rem(res + step, n_res)})
+
+    def near(step, turn):
+        slot = lax.rem(res + n_res - step, n_res) * n_seq + seq
+        return right_copy(slot, turn * n_res + step, {"seq": lax.rem(seq + turn, n_seq)})
+
     each(n_all, lambda step: left_copy(step).start())
-    each(n_src, lambda step: right_copy(step).start())
+    each(n_res, lambda step: far(step).start())
+    each(n_seq, lambda turn: near(0, turn).start())
     left_all[me] = left_send[src]
 
     w_copy.wait()
@@ -172,7 +179,14 @@
     for u in range(n_col // fold):
         taken = left_all[pl.ds(u * fold * n_src, fold * n_src)].astype(F32)
         left_flip[u] = taken.reshape(deep, rows * chans).T.astype(BF16)
-    each(n_src, lambda step: right_copy(step).wait())
+
+    def relay(step):
+        far(step).wait()
+        each(n_seq, lambda turn: near(step, turn).start())
+
+    each(n_res, relay)
+    for step in range(n_res):
+        each(n_seq, lambda turn: near(step, turn).wait())
 
     factor = 1.0 / float(seqs * n_src)
     for u in range(n_col // fold):

time: 16.1 us -> 15.5 us (0.963)
  Pallas kernels: 15.2 us -> 14.7 us
    pallas_call x1, Pallas kernels: 15.2 us -> 14.7 us  [per_device(): pl.pallas_call(functools.partial(kernel, dims), out_shape=pltpu.VMEM((n_c...]
where the time goes in v3:
time: 15.5 us; the launch traced here: 15.4 us
  Pallas kernels  14.7 us (95%)
  local copies, waits for them, and re-layouts  0.71 us (5%)
    pallas_call x1, Pallas kernels, per_device(): pl.pallas_call(functools.partial(kernel, dims), out_shape=pltpu.VMEM((n_c...  14.7 us
    unnamed x1, local copies, waits for them, and re-layouts  0.71 us

profile of v3, /device:TPU:0, one launch (start us, length us, event | category | flops | bytes accessed | tf_op | source)
XLA Modules:
  0.0 15.4 jit_solution(2651123518289455929)
XLA Ops:
  0.0 14.7 %shard_map.91 = bf16[2,8,64,128]{3,2,1,0:T(8,128)(2,1)S(1)} custom-call(bf16[8,64,256]{2,1,0:T(8,128)(2,1)} %msa.1, f32[1,256]{1,0:T(1,128)} %bitcast.9, f32[1,256]{1,0:T(1,128)} %bitcast.10, bf16[32,256]{1,0:T(8,128)(2,1)} %bitcast.7, f32[1,32]{1,0:T(1,128)} %bitcast.11, bf16[32,256]{1,0:T(8,128)(2,1)} %bitcast.8, f32[1,32]{1,0:T(1,128)} %bitcast.12, ...), custom_call_target="tpu_custom_call" | custom-call | tf_op jit(solution)/shard_map/pallas_call | solution.py:240
  14.7 0.7 %copy.11 = bf16[2,8,64,128]{3,2,1,0:T(8,128)(2,1)} copy(bf16[2,8,64,128]{3,2,1,0:T(8,128)(2,1)S(1)} %shard_map.91) | data formatting | bytes 524288

commit v4 on v3

--- a/solution.py
+++ b/solution.py
@@ -61,7 +61,6 @@
 ):
     n_res, n_col, n_seq, seqs, span, width, chans, pairs = dims
     n_src = n_res * n_seq
-    n_all = n_src * n_col
     fold = max(1, 128 // span)
     high = chans // fold
     rows = span // n_src
@@ -69,11 +68,18 @@
     group = outer.shape[2] // lanes
     res, col, seq = lax.axis_index("res"), lax.axis_index("col"), lax.axis_index("seq")
     src = res * n_seq + seq
-    me = col * n_src + src
-
-    def place(index):
-        at = lax.rem(index, n_src)
-        return {"res": at // n_seq, "col": index // n_src, "seq": lax.rem(at, n_seq)}
+
+    def place(at):
+        return {"res": at // n_seq, "seq": lax.rem(at, n_seq)}
+
+    def mates(step):
+        if n_res & (n_res - 1):
+            return lax.rem(res + step, n_res), lax.rem(res + n_res - step, n_res)
+        mate, bit = 0, 1
+        while bit < n_res:
+            mate = mate + (res // bit + step // bit) % 2 * bit
+            bit *= 2
+        return mate, mate
 
     def each(count, body):
         if count <= 16:
@@ -84,10 +90,11 @@
 
     barrier = pltpu.get_barrier_semaphore()
 
-    def greet(step):
-        pl.semaphore_signal(barrier, inc=1, device_id=place(lax.rem(me + step, n_all)), device_id_type=MESH)
-
-    each(n_all, greet)
+    def greet(to):
+        pl.semaphore_signal(barrier, inc=1, device_id=to, device_id_type=MESH)
+
+    each(n_src, lambda step: greet(place(lax.rem(src + step, n_src))))
+    each(n_col, lambda turn: greet({"col": lax.rem(col + turn, n_col)}))
     w_copy = pltpu.make_async_copy(w_hbm, w_vmem, w_sem)
     w_copy.start()
 
@@ -129,16 +136,26 @@
     total = total.reshape(n_src, seqs, rows * chans).astype(BF16)
     left_send[...] = total
 
-    pl.semaphore_wait(barrier, n_all - 1)
+    pl.semaphore_wait(barrier, n_src + n_col - 2)
 
     def left_copy(step):
-        to = lax.rem(me + step, n_all)
+        to = lax.rem(src + step, n_src)
         return pltpu.make_async_remote_copy(
-            src_ref=left_send.at[lax.rem(to, n_src)],
-            dst_ref=left_all.at[me],
+            src_ref=left_send.at[to],
+            dst_ref=left_all.at[col, src],
             send_sem=left_ssem.at[step],
             recv_sem=left_rsem.at[step],
             device_id=place(to),
+            device_id_type=MESH,
+        )
+
+    def across(turn):
+        return pltpu.make_async_remote_copy(
+            src_ref=left_all.at[col],
+            dst_ref=left_all.at[col],
+            send_sem=left_ssem.at[n_src + turn],
+            recv_sem=left_rsem.at[n_src + turn],
+            device_id={"col": lax.rem(col + turn, n_col)},
             device_id_type=MESH,
         )
 
@@ -153,16 +170,17 @@
         )
 
     def far(step):
-        return right_copy(src, step, {"res": lax.rem(res + step, n_res)})
+        return right_copy(src, step, {"res": mates(step)[0]})
 
     def near(step, turn):
-        slot = lax.rem(res + n_res - step, n_res) * n_seq + seq
+        slot = src if step is None else mates(step)[1] * n_seq + seq
+        step = 0 if step is None else step
         return right_copy(slot, turn * n_res + step, {"seq": lax.rem(seq + turn, n_seq)})
 
-    each(n_all, lambda step: left_copy(step).start())
+    each(n_src, lambda step: left_copy(step).start())
     each(n_res, lambda step: far(step).start())
-    each(n_seq, lambda turn: near(0, turn).start())
-    left_all[me] = left_send[src]
+    each(n_seq, lambda turn: near(None, turn).start())
+    left_all[col, src] = left_send[src]
 
     w_copy.wait()
     w_f32[...] = w_vmem[...].astype(F32)
@@ -174,18 +192,20 @@
         w_flip[:, pl.ds(at * chans, chunk * chans)] = taken.T.astype(BF16)
     offset = column_of(b_out[...], pairs)
 
-    each(n_all, lambda step: left_copy(step).wait())
-    deep = fold * n_src * seqs
-    for u in range(n_col // fold):
-        taken = left_all[pl.ds(u * fold * n_src, fold * n_src)].astype(F32)
-        left_flip[u] = taken.reshape(deep, rows * chans).T.astype(BF16)
-
+    each(n_src, lambda step: left_copy(step).wait())
+    each(n_col, lambda turn: across(turn).start())
     def relay(step):
         far(step).wait()
         each(n_seq, lambda turn: near(step, turn).start())
 
     each(n_res, relay)
-    for step in range(n_res):
+    each(n_col, lambda turn: across(turn).wait())
+    deep = fold * n_src * seqs
+    for u in range(n_col // fold):
+        taken = left_all[pl.ds(u * fold, fold)].astype(F32)
+        left_flip[u] = taken.reshape(deep, rows * chans).T.astype(BF16)
+    each(n_seq, lambda turn: near(None, turn).wait())
+    for step in range(1, n_res):
         each(n_seq, lambda turn: near(step, turn).wait())
 
     factor = 1.0 / float(seqs * n_src)
@@ -249,13 +269,13 @@
             pltpu.VMEM((seqs * span, 2 * chans), F32),
             pltpu.VMEM((lanes // 128, seqs * high, 128), F32),
             pltpu.VMEM((n_src, seqs, rows * chans), BF16),
-            pltpu.VMEM((n_src * n_col, seqs, rows * chans), BF16),
+            pltpu.VMEM((n_col, n_src, seqs, rows * chans), BF16),
             pltpu.VMEM((n_col // fold, rows * chans, deep), BF16),
             pltpu.VMEM((n_src, high, seqs, lanes), BF16),
             pltpu.VMEM((rows // group, chans * chans, group * lanes), BF16),
             pltpu.SemaphoreType.DMA,
-            pltpu.SemaphoreType.DMA((n_src * n_col,)),
-            pltpu.SemaphoreType.DMA((n_src * n_col,)),
+            pltpu.SemaphoreType.DMA((n_src + n_col,)),
+            pltpu.SemaphoreType.DMA((n_src + n_col,)),
             pltpu.SemaphoreType.DMA((n_src,)),
             pltpu.SemaphoreType.DMA((n_src,)),
         ],

time: 15.5 us -> 14.7 us (0.948)
  Pallas kernels: 14.7 us -> 13.9 us
    pallas_call x1, Pallas kernels: 14.7 us -> 13.9 us  [per_device(): pl.pallas_call(functools.partial(kernel, dims), out_shape=pltpu.VMEM((n_c...]
where the time goes in v4:
time: 14.7 us; the launch traced here: 14.6 us
  Pallas kernels  13.9 us (95%)
  local copies, waits for them, and re-layouts  0.71 us (5%)
    pallas_call x1, Pallas kernels, per_device(): pl.pallas_call(functools.partial(kernel, dims), out_shape=pltpu.VMEM((n_c...  13.9 us
    unnamed x1, local copies, waits for them, and re-layouts  0.71 us

profile of v4, /device:TPU:0, one launch (start us, length us, event | category | flops | bytes accessed | tf_op | source)
XLA Modules:
  0.0 14.6 jit_solution(17513381429453187801)
XLA Ops:
  0.0 13.9 %shard_map.91 = bf16[2,8,64,128]{3,2,1,0:T(8,128)(2,1)S(1)} custom-call(bf16[8,64,256]{2,1,0:T(8,128)(2,1)} %msa.1, f32[1,256]{1,0:T(1,128)} %bitcast.9, f32[1,256]{1,0:T(1,128)} %bitcast.10, bf16[32,256]{1,0:T(8,128)(2,1)} %bitcast.7, f32[1,32]{1,0:T(1,128)} %bitcast.11, bf16[32,256]{1,0:T(8,128)(2,1)} %bitcast.8, f32[1,32]{1,0:T(1,128)} %bitcast.12, ...), custom_call_target="tpu_custom_call" | custom-call | tf_op jit(solution)/shard_map/pallas_call | solution.py:260
  13.9 0.7 %copy.11 = bf16[2,8,64,128]{3,2,1,0:T(8,128)(2,1)} copy(bf16[2,8,64,128]{3,2,1,0:T(8,128)(2,1)S(1)} %shard_map.91) | data formatting | bytes 524288

commit v5 on v4

--- a/solution.py
+++ b/solution.py
@@ -178,7 +178,12 @@
         return right_copy(slot, turn * n_res + step, {"seq": lax.rem(seq + turn, n_seq)})
 
     each(n_src, lambda step: left_copy(step).start())
-    each(n_res, lambda step: far(step).start())
+    if n_res <= 16:
+        hops = {k: [abs((p ^ k) - p) for p in range(n_res)] for k in range(1, n_res)}
+        for step in sorted(hops, key=lambda k: (-sum(hops[k]), -min(hops[k]))):
+            far(step).start()
+    else:
+        each(n_res, lambda step: far(step).start())
     each(n_seq, lambda turn: near(None, turn).start())
     left_all[col, src] = left_send[src]
 

time: 14.7 us -> 14.6 us (level)
  Pallas kernels: 13.9 us -> 13.7 us
where the time goes in v5:
time: 14.6 us; the launch traced here: 14.4 us
  Pallas kernels  13.7 us (94%)
  local copies, waits for them, and re-layouts  0.71 us (5%)
    pallas_call x1, Pallas kernels, per_device(): pl.pallas_call(functools.partial(kernel, dims), out_shape=pltpu.VMEM((n_c...  13.7 us
    unnamed x1, local copies, waits for them, and re-layouts  0.71 us

profile of v5, /device:TPU:0, one launch (start us, length us, event | category | flops | bytes accessed | tf_op | source)
XLA Modules:
  0.0 14.4 jit_solution(7989215353076933678)
XLA Ops:
  0.0 13.7 %shard_map.91 = bf16[2,8,64,128]{3,2,1,0:T(8,128)(2,1)S(1)} custom-call(bf16[8,64,256]{2,1,0:T(8,128)(2,1)} %msa.1, f32[1,256]{1,0:T(1,128)} %bitcast.9, f32[1,256]{1,0:T(1,128)} %bitcast.10, bf16[32,256]{1,0:T(8,128)(2,1)} %bitcast.7, f32[1,32]{1,0:T(1,128)} %bitcast.11, bf16[32,256]{1,0:T(8,128)(2,1)} %bitcast.8, f32[1,32]{1,0:T(1,128)} %bitcast.12, ...), custom_call_target="tpu_custom_call" | custom-call | tf_op jit(solution)/shard_map/pallas_call | solution.py:265
  13.7 0.7 %copy.11 = bf16[2,8,64,128]{3,2,1,0:T(8,128)(2,1)} copy(bf16[2,8,64,128]{3,2,1,0:T(8,128)(2,1)S(1)} %shard_map.91) | data formatting | bytes 524288
